TPU v7x, 128 devices: a whole 4x4x4 slice. The times are simulated.
128 devices in a mesh: seq: 32 (over z, y, core), head: 4 (over x).
Axes of the slice: x: 4, y: 4, z: 4, core: 2. Of those that a mesh axis runs over, the one named last changes fastest.
Arguments:
- tokens: bfloat16 [98304, 768], P('seq'), may hold values from -6 to 6
- w_query: bfloat16 [768, 768], P(None, 'head'), may hold values from -0.21875 to 0.21875
- w_key: bfloat16 [768, 768], P(None, 'head'), may hold values from -0.21875 to 0.21875
- w_value: bfloat16 [768, 768], P(None, 'head'), may hold values from -0.21875 to 0.21875
- freq: float32 [64, 128], replicated, may hold values from -1.5 to 1.5
- w_out: bfloat16 [768, 768], replicated, may hold values from -0.21875 to 0.21875
- router: bfloat16 [768, 128], replicated, may hold values from -0.21875 to 0.21875
- w_in: bfloat16 [128, 768, 3072], P(('seq', 'head')), may hold values from -0.21875 to 0.21875
- w_down: bfloat16 [128, 3072, 768], P(('seq', 'head')), may hold values from -0.109375 to 0.109375
- picks: int32 [128, 128, 6], P(None, ('seq', 'head')), may hold values from 0 to 767, as said below
Outputs:
- layer_out: bfloat16 [98304, 768], P(('seq', 'head'))
Inputs may be any that keep to these rules, and one draw needn't show every extreme that they name: `picks`: for each expert and each source block the 6 picked rows are distinct.
All inputs are finite; a program needn't handle non-finite values.
Results may differ from a plain program's by a relative error of at most 0.017.
Values may be sent and summed in bfloat16 or wider, within the bound.
A program may use at most 128 MiB of HBM per device.

v0:
```python
import functools
import math

import jax
import jax.numpy as jnp
from jax import lax
from jax.experimental import pallas as pl
from jax.experimental.pallas import tpu as pltpu
from jax.sharding import Mesh
from jax.sharding import PartitionSpec as P

MESH = pl.DeviceIdType.MESH
AXES = ("z", "y", "c", "head")
HD = 64
CHUNK = 256
EPS = 1e-06
F32 = jnp.float32
BF16 = jnp.bfloat16

SCALE = 1.0 / math.sqrt(128.0)
ROOT = math.sqrt(2.0 * SCALE)
SIN = [ROOT * v for v in (3.141582022210377, -5.167142797933202, 2.541899038850396, -0.5546362211874226)]
COS = [
    ROOT * v
    for v in (
        0.9999999535200743,
        -4.93479286153638,
        4.0584119554710245,
        -1.3318803818997542,
        0.21969719133234294,
    )
]
ROUNDER = 12582912.0


def nt(a, b):
    return lax.dot_general(a, b, (((1,), (1,)), ((), ())), preferred_element_type=F32)


def nn(a, b):
    return lax.dot_general(a, b, (((1,), (0,)), ((), ())), preferred_element_type=F32)


def tn(a, b):
    return lax.dot_general(a, b, (((0,), (0,)), ((), ())), preferred_element_type=F32)


def waves(turns):
    r = turns - ((turns + ROUNDER) - ROUNDER)
    y = r * r
    a = r * (SIN[0] + y * (SIN[1] + y * (SIN[2] + y * SIN[3])))
    b = COS[0] + y * (COS[1] + y * (COS[2] + y * (COS[3] + y * COS[4])))
    return (SCALE - a * a).astype(BF16), (a * b).astype(BF16)


def feature_heads(x, wx, wf01, wf2):
    proj = nn(x, wx).astype(BF16)
    pair, last = proj[:, :128], proj[:, 128:]
    cos01, sin01 = waves(nn(jnp.concatenate([pair, pair], axis=1), wf01))
    cos2, sin2 = waves(nn(last, wf2))
    return (
        jnp.concatenate([cos01[:, :128], sin01[:, :128]], axis=1),
        jnp.concatenate([cos01[:, 128:], sin01[:, 128:]], axis=1),
        jnp.concatenate([cos2, sin2], axis=1),
    )


def attention_kernel(
    tok, wq, wk, wv, freq, out,
    xbuf, wqx, wkx, wvt, wf01, wf2, kf, qf, vt, before, intra, run, prefix,
    cs, cr, ys, yr, zs, zr, fs, fr, att,
    xsem, csem, ysend, yrecv, zsend, zrecv, hsend, hrecv,
):
    z, y, c, x = (lax.axis_index(a) for a in AXES)
    heads = 3
    chunks = xbuf.shape[0]
    per = chunks // 4

    def fetch(i):
        return pltpu.make_async_copy(
            tok.at[pl.ds(pl.multiple_of(i * CHUNK, CHUNK), CHUNK), :], xbuf.at[i], xsem.at[i]
        )

    @pl.loop(0, chunks)
    def _(i):
        fetch(i).start()

    core = (z, y, 1 - c, x)
    y_peers = [(z, y ^ k, c, x) for k in (1, 2, 3)]
    z_peers = [(z ^ k, y, c, x) for k in (1, 2, 3)]
    x_peers = [(z, y, c, x ^ k) for k in (1, 2, 3)]
    barrier = pltpu.get_barrier_semaphore()
    for peer in [core] + y_peers + z_peers + x_peers:
        pl.semaphore_signal(barrier, inc=1, device_id=peer, device_id_type=MESH)

    for src, dst in ((wq, wqx), (wk, wkx)):
        w = src[...]
        dst[:, :192] = w
        dst[:, 192:] = w[:, 128:192]
    wvt[...] = wv[...].T
    turns = freq[...] * (1.0 / (2.0 * math.pi))
    high = turns.astype(BF16)
    low = (turns - high.astype(F32)).astype(BF16)
    wf01[...] = jnp.zeros_like(wf01)
    wf01[0:64, 0:128] = high
    wf01[64:128, 128:256] = high
    wf01[128:192, 0:128] = low
    wf01[192:256, 128:256] = low
    wf2[0:64, :] = high
    wf2[64:128, :] = low
    run[...] = jnp.zeros_like(run)

    @pl.loop(0, chunks)
    def _(i):
        fetch(i).wait()
        xs = xbuf[i]
        vals = nt(wvt[...], xs).astype(BF16)
        vt[i] = vals
        feats = feature_heads(xs, wkx[...], wf01[...], wf2[...])
        before[i] = run[...]
        for h in range(heads):
            kf[h, i] = feats[h]
            run[h * HD : (h + 1) * HD, :] += nn(vals[h * HD : (h + 1) * HD, :], feats[h])

    def send(src, dst, ssem, rsem, peer):
        return pltpu.make_async_remote_copy(
            src_ref=src, dst_ref=dst, send_sem=ssem, recv_sem=rsem, device_id=peer, device_id_type=MESH
        )

    half = cs.shape[0] // 2
    mine = pl.ds(pl.multiple_of(c * half, half), half)
    other = pl.ds(pl.multiple_of((1 - c) * half, half), half)
    c_copy = send(cs, cr, csem.at[0], csem.at[1], core)
    y_copies = [send(ys, yr.at[y], ysend.at[k], yrecv.at[k], y_peers[k]) for k in range(3)]
    z_copies = [send(zs, zr.at[z], zsend.at[k], zrecv.at[k], z_peers[k]) for k in range(3)]
    f_copy = send(fs, fr, csem.at[2], csem.at[3], core)

    pl.semaphore_wait(barrier, 10)
    cs[...] = run[...].astype(BF16)
    c_copy.start()

    def scan_pieces(pieces, index):
        inside = jnp.zeros(pieces.shape[1:], F32)
        total = jnp.zeros(pieces.shape[1:], F32)
        for k in range(4):
            piece = pieces[k].astype(F32)
            inside = inside + jnp.where(k < index, piece, 0.0)
            total = total + piece
        return inside, total

    rows = lax.broadcasted_iota(jnp.int32, (CHUNK, CHUNK), 0)
    columns = lax.broadcasted_iota(jnp.int32, (CHUNK, CHUNK), 1)
    causal = rows <= columns

    @pl.loop(0, chunks)
    def _(i):
        @pl.when(i == 2)
        def _():
            c_copy.wait()
            ys[...] = (run[mine, :] + cr[mine, :].astype(F32)).astype(BF16)
            yr[y] = ys[...]
            for copy in y_copies:
                copy.start()

        @pl.when(i == 5)
        def _():
            for copy in y_copies:
                copy.wait()
            inside, total = scan_pieces(yr, y)
            prefix[mine, :] = inside
            zs[...] = total.astype(BF16)
            zr[z] = zs[...]
            for copy in z_copies:
                copy.start()

        @pl.when(i == 9)
        def _():
            for copy in z_copies:
                copy.wait()
            inside, _ = scan_pieces(zr, z)
            total = inside + prefix[mine, :]
            prefix[mine, :] = total
            fs[...] = total.astype(BF16)
            f_copy.start()

        feats = feature_heads(xbuf[i], wqx[...], wf01[...], wf2[...])
        for h in range(heads):
            qf[h, i] = feats[h]
            scores = nt(kf[h, i], feats[h])
            scores = jnp.where(causal, scores, 0.0).astype(BF16)
            intra[i, h * HD : (h + 1) * HD, :] = nn(vt[i, h * HD : (h + 1) * HD, :], scores)

    f_copy.wait()
    prefix[other, :] = fr[...].astype(F32)
    prefix[...] += jnp.where(c == 1, cr[...].astype(F32), 0.0)

    def finish(i, j, dst):
        state = (prefix[...] + before[i]).astype(BF16)
        for h in range(heads):
            band = slice(h * HD, (h + 1) * HD)
            raw = intra[i, band, :] + nt(state[band, :], qf[h, i])
            mean = jnp.mean(raw * raw, axis=0, keepdims=True)
            dst[band, j * CHUNK : (j + 1) * CHUNK] = (raw * lax.rsqrt(mean + EPS)).astype(BF16)

    h_copies = [send(att.at[x ^ k], out.at[x], hsend.at[k - 1], hrecv.at[k - 1], x_peers[k - 1]) for k in (1, 2, 3)]
    for k in (1, 2, 3):
        for j in range(per):
            finish((x ^ k) * per + j, j, att.at[x ^ k])
        h_copies[k - 1].start()
    for j in range(per):
        finish(x * per + j, j, out.at[x])
    for copy in h_copies:
        copy.wait()


def attention(tokens, w_query, w_key, w_value, freq):
    total, width = tokens.shape
    chunks = total // CHUNK
    cols = w_query.shape[1]
    vmem = pl.BlockSpec(memory_space=pltpu.VMEM)
    dma = pltpu.SemaphoreType.DMA
    return pl.pallas_call(
        attention_kernel,
        name="attention",
        out_shape=jax.ShapeDtypeStruct((4, cols, total // 4), BF16),
        in_specs=[pl.BlockSpec(memory_space=pl.ANY)] + [vmem] * 4,
        out_specs=vmem,
        scratch_shapes=[
            pltpu.VMEM((chunks, CHUNK, width), BF16),
            pltpu.VMEM((width, 256), BF16),
            pltpu.VMEM((width, 256), BF16),
            pltpu.VMEM((cols, width), BF16),
            pltpu.VMEM((256, 256), BF16),
            pltpu.VMEM((128, 128), BF16),
            pltpu.VMEM((3, chunks, CHUNK, 256), BF16),
            pltpu.VMEM((3, chunks, CHUNK, 256), BF16),
            pltpu.VMEM((chunks, cols, CHUNK), BF16),
            pltpu.VMEM((chunks, cols, 256), F32),
            pltpu.VMEM((chunks, cols, CHUNK), F32),
            pltpu.VMEM((cols, 256), F32),
            pltpu.VMEM((cols, 256), F32),
            pltpu.VMEM((cols, 256), BF16),
            pltpu.VMEM((cols, 256), BF16),
            pltpu.VMEM((cols // 2, 256), BF16),
            pltpu.VMEM((4, cols // 2, 256), BF16),
            pltpu.VMEM((cols // 2, 256), BF16),
            pltpu.VMEM((4, cols // 2, 256), BF16),
            pltpu.VMEM((cols // 2, 256), BF16),
            pltpu.VMEM((cols // 2, 256), BF16),
            pltpu.VMEM((4, cols, total // 4), BF16),
            dma((chunks,)),
            dma((4,)),
            dma((3,)),
            dma((3,)),
            dma((3,)),
            dma((3,)),
            dma((3,)),
            dma((3,)),
        ],
        compiler_params=pltpu.CompilerParams(
            collective_id=0, has_side_effects=True, vmem_limit_bytes=56 << 20
        ),
    )(tokens, w_query, w_key, w_value, freq)


SLOT = 8
GROUP = 32


def experts_kernel(
    cap, tok, heads, w_out, router, pick_col, pick_row, w_in, w_down, out,
    resid, hid, gates, first, second, outgoing, arrived, inner, result, returned,
    insem, osem, asem, rsem, bsem, lsem,
):
    z, y, c, x = (lax.axis_index(a) for a in AXES)
    me = ((z * 4 + y) * 2 + c) * 4 + x
    tokens, width = hid.shape
    span = GROUP * SLOT

    in_copy = pltpu.make_async_copy(
        tok.at[pl.ds(pl.multiple_of(x * tokens, tokens), tokens), :], resid, insem.at[0]
    )
    first_copy = pltpu.make_async_copy(w_in.at[0], first, insem.at[1])
    second_copy = pltpu.make_async_copy(w_down.at[0], second, insem.at[2])
    in_copy.start()
    first_copy.start()
    second_copy.start()
    returned[...] = jnp.zeros_like(returned)

    def peer(g, j):
        return (z ^ g, y ^ (j >> 3), c ^ ((j >> 2) & 1), x ^ (j & 3))

    def flat(p):
        return ((p[0] * 4 + p[1]) * 2 + p[2]) * 4 + p[3]

    barrier = pltpu.get_barrier_semaphore()

    def greet(g, j):
        pl.semaphore_signal(barrier, inc=1, device_id=peer(g, j), device_id_type=MESH)

    for g in range(4):

        @pl.loop(1 if g == 0 else 0, GROUP)
        def _(j, g=g):
            greet(g, j)

    in_copy.wait()
    hid[...] = (resid[...].astype(F32) + tn(heads[...], w_out[...])).astype(BF16)

    def gather(zz):
        base = pl.multiple_of(zz * span, span)
        picked = pick_col[pl.ds(base, span), :] == lax.broadcasted_iota(jnp.int32, (span, tokens), 1)
        rows = nn(picked.astype(F32).astype(BF16), hid[...])
        outgoing[pl.ds(zz * GROUP, GROUP)] = rows.reshape(GROUP, SLOT, width).astype(BF16)

    def exchange(src, dst, ssem, rsem, g, there=True):
        def one(j):
            p = peer(g, j)
            pltpu.make_async_remote_copy(
                src_ref=src.at[flat(p), pl.ds(0, cap)],
                dst_ref=dst.at[me, pl.ds(0, cap)],
                send_sem=ssem.at[g],
                recv_sem=rsem.at[g],
                device_id=p,
                device_id_type=MESH,
            ).start()

        @pl.loop(1 if g == 0 else 0, GROUP)
        def _(j):
            one(j)

    def drain(src, dst, ssem, rsem, g, sent):
        n = GROUP - 1 if g == 0 else GROUP
        copy = pltpu.make_async_remote_copy(
            src_ref=src.at[pl.ds(0, n), pl.ds(0, cap)],
            dst_ref=dst.at[pl.ds(0, n), pl.ds(0, cap)],
            send_sem=ssem.at[g],
            recv_sem=rsem.at[g],
            device_id=peer(1, 0),
            device_id_type=MESH,
        )
        if sent:
            copy.wait_send()
        else:
            copy.wait_recv()

    own_out = pltpu.make_async_copy(outgoing.at[me], arrived.at[me], lsem.at[0])
    own_back = pltpu.make_async_copy(result.at[me], returned.at[me], lsem.at[1])

    pl.semaphore_wait(barrier, 127)
    for g in (1, 2, 3, 0):
        gather(z ^ g)
        if g == 0:
            own_out.start()
        exchange(outgoing, arrived, osem, asem, g)

    gate = jax.nn.sigmoid(nn(hid[...], router[...])).astype(BF16)
    experts = gate.shape[1]
    slots = experts * SLOT
    spread = (
        lax.broadcasted_iota(jnp.int32, (experts, slots), 1) // SLOT
        == lax.broadcasted_iota(jnp.int32, (experts, slots), 0)
    )
    wide = nn(gate, spread.astype(F32).astype(BF16))
    mine = lax.broadcasted_iota(jnp.int32, (tokens, slots), 0) == pick_row[...]
    gates[...] = jnp.where(mine, wide, 0.0).astype(BF16)

    first_copy.wait()
    second_copy.wait()
    own_out.wait()
    for g in (1, 2, 3, 0):
        drain(outgoing, arrived, osem, asem, g, False)
        zz = z ^ g
        group = pl.ds(pl.multiple_of(zz * GROUP, GROUP), GROUP)
        rows = arrived[group].astype(F32).reshape(span, width).astype(BF16)
        for part in range(6):
            band = slice(part * 512, (part + 1) * 512)
            inner[:, band] = jax.nn.gelu(nn(rows, first[:, band]), approximate=True).astype(BF16)
        result[group] = nn(inner[...], second[...]).reshape(GROUP, SLOT, width).astype(BF16)
        if g == 0:
            own_back.start()
        exchange(result, returned, bsem, rsem, g)

    own_back.wait()
    for g in (1, 2, 3, 0):
        drain(outgoing, arrived, osem, asem, g, True)
        drain(result, returned, bsem, rsem, g, True)
        drain(result, returned, bsem, rsem, g, False)
    back = returned[...].astype(F32).reshape(slots, width).astype(BF16)
    out[...] = (hid[...].astype(F32) + nn(gates[...], back)).astype(BF16)


def experts(tokens, heads, w_out, router, picks, w_in, w_down):
    width = tokens.shape[1]
    count, _, cap = picks.shape
    rows = heads.shape[1]
    ff = w_in.shape[2]
    padded = jnp.pad(picks.reshape(count, cap), ((0, 0), (0, SLOT - cap)), constant_values=-1)
    vmem = pl.BlockSpec(memory_space=pltpu.VMEM)
    hbm = pl.BlockSpec(memory_space=pl.ANY)
    dma = pltpu.SemaphoreType.DMA
    slots = pltpu.VMEM((count, SLOT, width), BF16)
    return pl.pallas_call(
        functools.partial(experts_kernel, cap),
        name="experts",
        out_shape=jax.ShapeDtypeStruct((rows, width), BF16),
        in_specs=[hbm, vmem, vmem, vmem, vmem, vmem, hbm, hbm],
        out_specs=vmem,
        scratch_shapes=[
            pltpu.VMEM((rows, width), BF16),
            pltpu.VMEM((rows, width), BF16),
            pltpu.VMEM((rows, count * SLOT), BF16),
            pltpu.VMEM((width, ff), BF16),
            pltpu.VMEM((ff, width), BF16),
            slots,
            slots,
            pltpu.VMEM((GROUP * SLOT, ff), BF16),
            slots,
            slots,
            dma((3,)),
            dma((4,)),
            dma((4,)),
            dma((4,)),
            dma((4,)),
            dma((2,)),
        ],
        compiler_params=pltpu.CompilerParams(
            collective_id=1, has_side_effects=True, vmem_limit_bytes=56 << 20
        ),
    )(tokens, heads, w_out, router, padded.reshape(-1, 1), padded.reshape(1, -1), w_in, w_down)


def per_device(tokens, w_query, w_key, w_value, freq, w_out, router, w_in, w_down, picks):
    heads = attention(tokens, w_query, w_key, w_value, freq)
    heads = heads.reshape(-1, heads.shape[2])
    return experts(tokens, heads, w_out, router, picks, w_in, w_down)


def solution(mesh):
    split = Mesh(mesh.devices.reshape(4, 4, 2, mesh.shape["head"]), AXES)
    seq = AXES[:3]
    in_specs = (
        P(seq, None),
        P(None, "head"),
        P(None, "head"),
        P(None, "head"),
        P(),
        P(),
        P(),
        P(AXES, None, None),
        P(AXES, None, None),
        P(None, AXES, None),
    )
    return jax.shard_map(
        per_device, mesh=split, in_specs=in_specs, out_specs=P(AXES, None), check_vma=False
    )
```

profile of v0, /device:TPU:1, one launch (start us, length us, event | category | flops | bytes accessed | tf_op | source)
XLA Modules:
  0.0 110.0 jit_solution(10918589517447137079)
XLA Ops:
  0.0 0.0 copy-start
  0.0 0.8 copy.24
  0.8 0.7 reshape.15.pick_row
  1.5 1.9 %copy.16.wq = bf16[768,192]{1,0:T(8,128)(2,1)} copy(bf16[768,192]{0,1:T(8,128)(2,1)} %param.11) | data formatting | bytes 589824 | tf_op args[1]
  3.4 1.9 %copy.17.wk = bf16[768,192]{1,0:T(8,128)(2,1)} copy(bf16[768,192]{0,1:T(8,128)(2,1)} %param.12) | data formatting | bytes 589824 | tf_op args[2]
  5.3 0.0 copy-done
  5.3 0.9 copy.18.wv
  6.2 46.8 %attention.1 = bf16[4,192,768]{2,1,0:T(8,128)(2,1)} custom-call(bf16[3072,768]{1,0:T(8,128)(2,1)} %tok.3, bf16[768,192]{1,0:T(8,128)(2,1)} %copy.16.wq, bf16[768,192]{1,0:T(8,128)(2,1)} %copy.17.wk, bf16[768,192]{1,0:T(8,128)(2,1)} %copy.18.wv, f32[64,128]{1,0:T(8,128)} %freq.1), custom_call_target="tpu_custom_call" | custom-call | tf_op jit(solution)/shard_map/attention/pallas_call | solution.py:222
  53.1 1.0 reshape.16.pick_col
  54.1 53.6 %experts.1 = bf16[768,768]{1,0:T(8,128)(2,1)} custom-call(bf16[3072,768]{1,0:T(8,128)(2,1)} %tok.3, bf16[768,768]{1,0:T(8,128)(2,1)} %bitcast.3, bf16[768,768]{1,0:T(8,128)(2,1)} %w_out.1, bf16[768,128]{1,0:T(8,128)(2,1)} %router.1, s32[1024,1]{1,0:T(8,128)} %reshape.16.pick_col, s32[1,1024]{1,0:T(1,128)} %reshape.15.pick_row, bf16[1,768,3072]{2,1,0:T(8,128)(2,1)} %w_in.1, ...), custom_call_target="tpu_custom_call" | custom-call | tf_op jit(solution)/shard_map/experts/pallas_call | solution.py:403
  107.7 2.4 %copy.26 = bf16[768,768]{1,0:T(8,128)(2,1)} copy(bf16[768,768]{1,0:T(8,128)(2,1)} %experts.1) | data formatting | bytes 2359296
  (1 shorter events, 0.0 us)
Async XLA Ops:
  0.0 5.3 %copy-start = (bf16[768,192]{0,1:T(8,128)(2,1)S(1)}, bf16[768,192]{0,1:T(8,128)(2,1)}, u32[]{:S(2)}) copy-start(bf16[768,192]{0,1:T(8,128)(2,1)} %param.13) | copy-start | bytes 884740
where the time goes:
time: 110 us
  Pallas kernels  100 us (91%)
  local copies, waits for them, and re-layouts  9.56 us (9%)
    pallas_call x1, Pallas kernels, experts(): pl.pallas_call(functools.partial(experts_kernel, cap), name='experts', ou...  53.6 us
    pallas_call x1, Pallas kernels, attention(): pl.pallas_call(attention_kernel, name='attention', out_shape=jax.ShapeDty...  46.8 us
    unnamed x7, local copies, waits for them, and re-layouts  7.89 us

commit v1 on v0

v1 whole, which is shorter than its diff:
```python
import functools
import math

import jax
import jax.numpy as jnp
from jax import lax
from jax.experimental import pallas as pl
from jax.experimental.pallas import tpu as pltpu
from jax.sharding import Mesh
from jax.sharding import PartitionSpec as P

MESH = pl.DeviceIdType.MESH
AXES = ("z", "y", "c", "head")
HD = 64
CHUNK = 256
EPS = 1e-06
F32 = jnp.float32
BF16 = jnp.bfloat16

SCALE = 1.0 / math.sqrt(128.0)
ROOT = math.sqrt(2.0 * SCALE)
SIN = [ROOT * v for v in (3.141582022210377, -5.167142797933202, 2.541899038850396, -0.5546362211874226)]
COS = [
    ROOT * v
    for v in (
        0.9999999535200743,
        -4.93479286153638,
        4.0584119554710245,
        -1.3318803818997542,
        0.21969719133234294,
    )
]
ROUNDER = 12582912.0


def nt(a, b):
    return lax.dot_general(a, b, (((1,), (1,)), ((), ())), preferred_element_type=F32)


def nn(a, b):
    return lax.dot_general(a, b, (((1,), (0,)), ((), ())), preferred_element_type=F32)


def tn(a, b):
    return lax.dot_general(a, b, (((0,), (0,)), ((), ())), preferred_element_type=F32)


def waves(turns):
    r = turns - ((turns + ROUNDER) - ROUNDER)
    y = r * r
    a = r * (SIN[0] + y * (SIN[1] + y * (SIN[2] + y * SIN[3])))
    b = COS[0] + y * (COS[1] + y * (COS[2] + y * (COS[3] + y * COS[4])))
    return (SCALE - a * a).astype(BF16), (a * b).astype(BF16)


def feature_heads(x, wx, wf01, wf2):
    proj = nt(x, wx).astype(BF16)
    pair, last = proj[:, :128], proj[:, 128:]
    cos01, sin01 = waves(nn(jnp.concatenate([pair, pair], axis=1), wf01))
    cos2, sin2 = waves(nn(last, wf2))
    return (
        jnp.concatenate([cos01[:, :128], sin01[:, :128]], axis=1),
        jnp.concatenate([cos01[:, 128:], sin01[:, 128:]], axis=1),
        jnp.concatenate([cos2, sin2], axis=1),
    )


SLOT = 8
GROUP = 32
HOPS = (0, 1, 2, 1)


def message_order():
    found = []
    for core in range(2):
        for k in range(64):
            a = k & 3
            b = ((k >> 2) + a) & 3
            d = ((k >> 4) + a + b) & 3
            found.append((-(HOPS[a] + HOPS[b] + HOPS[d]), k, -core, (a, b, core, d)))
    found.sort()
    return [f[3] for f in found]


ORDER = message_order()


def flat(p):
    return ((p[0] * 4 + p[1]) * 2 + p[2]) * 4 + p[3]


def layer_kernel(
    cap, tok, wq, wk, wv, freq, w_out, router, picks, w_in, w_down, out,
    xbuf, wqx, wkx, wf01, wf2, kf, qf, vt, before, intra, run, prefix,
    cs, cr, ys, yr, zs, zr, fs, fr, att, slabs,
    wo, acc, hid, onehot, gates, first, second, outgoing, arrived, inner, result, returned,
    xsem, csem, ysend, yrecv, zsend, zrecv, hsend, hrecv, insem, osem, asem, rsem, bsem, lsem,
):
    z, y, c, x = (lax.axis_index(a) for a in AXES)
    heads = 3
    chunks = xbuf.shape[0]
    per = chunks // 4
    tokens, width = hid.shape
    slots = onehot.shape[0]
    count = slots // SLOT
    span = GROUP * SLOT

    def peer(offset):
        return (z ^ offset[0], y ^ offset[1], c ^ offset[2], x ^ offset[3])

    def fetch(i):
        return pltpu.make_async_copy(
            tok.at[pl.ds(pl.multiple_of(i * CHUNK, CHUNK), CHUNK), :], xbuf.at[i], xsem.at[i]
        )

    @pl.loop(0, chunks)
    def _(i):
        fetch(i).start()

    wo_copy = pltpu.make_async_copy(w_out, wo, insem.at[0])
    first_copy = pltpu.make_async_copy(w_in.at[0], first, insem.at[1])
    second_copy = pltpu.make_async_copy(w_down.at[0], second, insem.at[2])

    returned[...] = jnp.zeros_like(returned)
    barrier = pltpu.get_barrier_semaphore()

    @pl.loop(1, 128)
    def _(k):
        pl.semaphore_signal(
            barrier,
            inc=1,
            device_id=(z ^ (k & 3), y ^ ((k >> 2) & 3), c ^ (k >> 6), x ^ ((k >> 4) & 3)),
            device_id_type=MESH,
        )

    for src, dst in ((wq, wqx), (wk, wkx)):
        dst[:192, :] = src[...]
        dst[192:, :] = src[128:192, :]
    turns = freq[...] * (1.0 / (2.0 * math.pi))
    high = turns.astype(BF16)
    low = (turns - high.astype(F32)).astype(BF16)
    wf01[...] = jnp.zeros_like(wf01)
    wf01[0:64, 0:128] = high
    wf01[64:128, 128:256] = high
    wf01[128:192, 0:128] = low
    wf01[192:256, 128:256] = low
    wf2[0:64, :] = high
    wf2[64:128, :] = low
    run[...] = jnp.zeros_like(run)

    @pl.loop(0, chunks // STEP)
    def _(p):
        for i in [p * STEP + s for s in range(STEP)]:
            fetch(i).wait()
        for i in [p * STEP + s for s in range(STEP)]:
            xs = xbuf[i]
            vals = nt(wv[...], xs).astype(BF16)
            vt[i] = vals
            feats = feature_heads(xs, wkx[...], wf01[...], wf2[...])
            before[i] = run[...]
            for h in range(heads):
                kf[h, i] = feats[h]
                run[h * HD : (h + 1) * HD, :] += nn(vals[h * HD : (h + 1) * HD, :], feats[h])

    def send(src, dst, ssem, rsem, to):
        return pltpu.make_async_remote_copy(
            src_ref=src, dst_ref=dst, send_sem=ssem, recv_sem=rsem, device_id=to, device_id_type=MESH
        )

    core = (z, y, 1 - c, x)
    y_peers = [(z, y ^ k, c, x) for k in (1, 2, 3)]
    z_peers = [(z ^ k, y, c, x) for k in (1, 2, 3)]
    half = cs.shape[0] // 2
    mine = pl.ds(pl.multiple_of(c * half, half), half)
    other = pl.ds(pl.multiple_of((1 - c) * half, half), half)
    c_copy = send(cs, cr, csem.at[0], csem.at[1], core)
    y_copies = [send(ys, yr.at[y], ysend.at[k], yrecv.at[k], y_peers[k]) for k in range(3)]
    z_copies = [send(zs, zr.at[z], zsend.at[k], zrecv.at[k], z_peers[k]) for k in range(3)]
    f_copy = send(fs, fr, csem.at[2], csem.at[3], core)

    cs[...] = run[...].astype(BF16)
    pl.semaphore_wait(barrier, 127)
    c_copy.start()
    wo_copy.start()
    first_copy.start()
    second_copy.start()

    def scan_pieces(pieces, index):
        inside = jnp.zeros(pieces.shape[1:], F32)
        total = jnp.zeros(pieces.shape[1:], F32)
        for k in range(4):
            piece = pieces[k].astype(F32)
            inside = inside + jnp.where(k < index, piece, 0.0)
            total = total + piece
        return inside, total

    rows = lax.broadcasted_iota(jnp.int32, (CHUNK, CHUNK), 0)
    columns = lax.broadcasted_iota(jnp.int32, (CHUNK, CHUNK), 1)
    causal = rows <= columns

    @pl.loop(0, chunks // STEP)
    def _(p):
        @pl.when(p == 1)
        def _():
            c_copy.wait()
            ys[...] = (run[mine, :] + cr[mine, :].astype(F32)).astype(BF16)
            yr[y] = ys[...]
            for copy in y_copies:
                copy.start()

        @pl.when(p == Y_DONE)
        def _():
            for copy in y_copies:
                copy.wait()
            inside, total = scan_pieces(yr, y)
            prefix[mine, :] = inside
            zs[...] = total.astype(BF16)
            zr[z] = zs[...]
            for copy in z_copies:
                copy.start()

        for i in [p * STEP + s for s in range(STEP)]:
            feats = feature_heads(xbuf[i], wqx[...], wf01[...], wf2[...])
            for h in range(heads):
                qf[h, i] = feats[h]
                scores = nt(kf[h, i], feats[h])
                scores = jnp.where(causal, scores, 0.0).astype(BF16)
                intra[i, h * HD : (h + 1) * HD, :] = nn(vt[i, h * HD : (h + 1) * HD, :], scores)

    for copy in z_copies:
        copy.wait()
    inside, _ = scan_pieces(zr, z)
    total = inside + prefix[mine, :]
    prefix[mine, :] = total
    fs[...] = total.astype(BF16)
    f_copy.start()
    f_copy.wait()
    prefix[other, :] = fr[...].astype(F32)
    prefix[...] += jnp.where(c == 1, cr[...].astype(F32), 0.0)

    def finish(i, j, dst):
        state = (prefix[...] + before[i]).astype(BF16)
        for h in range(heads):
            band = slice(h * HD, (h + 1) * HD)
            raw = intra[i, band, :] + nt(state[band, :], qf[h, i])
            mean = jnp.mean(raw * raw, axis=0, keepdims=True)
            dst[band, j * CHUNK : (j + 1) * CHUNK] = (raw * lax.rsqrt(mean + EPS)).astype(BF16)

    h_copies = {}
    for j in range(per):
        for k in (2, 1, 3):
            finish((x ^ k) * per + j, j, att.at[x ^ k])
            part = (slice(None), slice(j * CHUNK, (j + 1) * CHUNK))
            h_copies[k, j] = send(
                att.at[(x ^ k, *part)],
                slabs.at[(x, *part)],
                hsend.at[(k - 1) * per + j],
                hrecv.at[(k - 1) * per + j],
                (z, y, c, x ^ k),
            )
            h_copies[k, j].start()
    for j in range(per):
        finish(x * per + j, j, slabs.at[x])

    numbers = jnp.concatenate([picks[...].reshape(cap, count), jnp.full((SLOT - cap, count), -16, jnp.int32)], axis=0)
    big = (numbers >> 4).astype(F32).astype(BF16)
    small = (numbers & 15).astype(F32).astype(BF16)
    tall = lax.broadcasted_iota(jnp.int32, (slots, count), 0) >> 3
    tall = (tall == lax.broadcasted_iota(jnp.int32, (slots, count), 1)).astype(F32).astype(BF16)
    places = nt(tall, big) * 16.0 + nt(tall, small)
    place = lax.broadcasted_iota(jnp.int32, (slots, SLOT), 0) & (SLOT - 1)
    place = place == lax.broadcasted_iota(jnp.int32, (slots, SLOT), 1)
    pick_col = jnp.sum(jnp.where(place, places, 0.0), axis=1, keepdims=True).astype(jnp.int32)
    for b in range(slots // span):
        band = slice(b * span, (b + 1) * span)
        picked = pick_col[band, :] == lax.broadcasted_iota(jnp.int32, (span, tokens), 1)
        onehot[band, :] = picked.astype(F32).astype(BF16)
    wide = lax.broadcasted_iota(jnp.int32, (count, slots), 1) >> 3
    wide = (wide == lax.broadcasted_iota(jnp.int32, (count, slots), 0)).astype(F32).astype(BF16)
    places = nn(big, wide) * 16.0 + nn(small, wide)
    place = lax.broadcasted_iota(jnp.int32, (SLOT, slots), 1) & (SLOT - 1)
    place = place == lax.broadcasted_iota(jnp.int32, (SLOT, slots), 0)
    pick_row = jnp.sum(jnp.where(place, places, 0.0), axis=0, keepdims=True).astype(jnp.int32)

    def project(k):
        band = pl.ds(pl.multiple_of((x ^ k) * 192, 192), 192)
        return tn(slabs[x ^ k], wo[band, :])

    wo_copy.wait()
    resid = jnp.concatenate([xbuf[x * per + j] for j in range(per)], axis=0)
    acc[...] = resid.astype(F32) + project(0)
    for k in (1, 3):
        for j in range(per):
            h_copies[k, j].wait()
        acc[...] += project(k)
    for j in range(per):
        h_copies[2, j].wait()
    hid[...] = (acc[...] + project(2)).astype(BF16)

    me = flat((z, y, c, x))

    def drain(src, dst, ssem, rsem, g, sent):
        n = GROUP - 1 if g == 3 else GROUP
        copy = send(
            src.at[pl.ds(0, n), pl.ds(0, cap)],
            dst.at[pl.ds(0, n), pl.ds(0, cap)],
            ssem.at[g],
            rsem.at[g],
            peer(ORDER[0]),
        )
        if sent:
            copy.wait_send()
        else:
            copy.wait_recv()

    own_out = pltpu.make_async_copy(outgoing.at[me], arrived.at[count - 1], lsem.at[0])
    own_back = pltpu.make_async_copy(result.at[count - 1], returned.at[me], lsem.at[1])

    for b in range(slots // span):
        rows = nn(onehot[b * span : (b + 1) * span, :], hid[...])
        outgoing[b * GROUP : (b + 1) * GROUP] = rows.reshape(GROUP, SLOT, width).astype(BF16)
    for i in range(count - 1):
        p = peer(ORDER[i])
        g = i // GROUP
        send(
            outgoing.at[flat(p), pl.ds(0, cap)], arrived.at[i, pl.ds(0, cap)], osem.at[g], asem.at[g], p
        ).start()
    own_out.start()

    gate = jax.nn.sigmoid(nn(hid[...], router[...])).astype(BF16)
    matched = lax.broadcasted_iota(jnp.int32, (tokens, slots), 0) == pick_row
    gates[...] = jnp.where(matched, nn(gate, wide), 0.0).astype(BF16)

    first_copy.wait()
    second_copy.wait()
    own_out.wait()
    for g in range(4):
        drain(outgoing, arrived, osem, asem, g, False)
        group = slice(g * GROUP, (g + 1) * GROUP)
        rows = arrived[group].astype(F32).reshape(span, width).astype(BF16)
        for part in range(6):
            band = slice(part * 512, (part + 1) * 512)
            inner[:, band] = jax.nn.gelu(nn(rows, first[:, band]), approximate=True).astype(BF16)
        result[group] = nn(inner[...], second[...]).reshape(GROUP, SLOT, width).astype(BF16)
        for i in range(g * GROUP, min((g + 1) * GROUP, count - 1)):
            send(
                result.at[i, pl.ds(0, cap)], returned.at[me, pl.ds(0, cap)], bsem.at[g], rsem.at[g], peer(ORDER[i])
            ).start()
    own_back.start()
    own_back.wait()
    for g in range(4):
        drain(outgoing, arrived, osem, asem, g, True)
        drain(result, returned, bsem, rsem, g, True)
        drain(result, returned, bsem, rsem, g, False)
    back = returned[...].astype(F32).reshape(slots, width).astype(BF16)
    out[...] = (hid[...].astype(F32) + nn(gates[...], back)).astype(BF16)


STEP = 2
Y_DONE = 4


def per_device(tokens, w_query, w_key, w_value, freq, w_out, router, w_in, w_down, picks):
    total, width = tokens.shape
    chunks = total // CHUNK
    cols = w_query.shape[1]
    own = total // 4
    count, _, cap = picks.shape
    ff = w_in.shape[2]
    slots = count * SLOT
    vmem = pl.BlockSpec(memory_space=pltpu.VMEM)
    hbm = pl.BlockSpec(memory_space=pl.ANY)
    dma = pltpu.SemaphoreType.DMA
    buf = pltpu.VMEM
    return pl.pallas_call(
        functools.partial(layer_kernel, cap),
        name="layer",
        out_shape=jax.ShapeDtypeStruct((own, width), BF16),
        in_specs=[hbm] + [vmem] * 4 + [hbm] + [vmem] * 2 + [hbm] * 2,
        out_specs=vmem,
        scratch_shapes=[
            buf((chunks, CHUNK, width), BF16),
            buf((256, width), BF16),
            buf((256, width), BF16),
            buf((256, 256), BF16),
            buf((128, 128), BF16),
            buf((3, chunks, CHUNK, 256), BF16),
            buf((3, chunks, CHUNK, 256), BF16),
            buf((chunks, cols, CHUNK), BF16),
            buf((chunks, cols, 256), F32),
            buf((chunks, cols, CHUNK), F32),
            buf((cols, 256), F32),
            buf((cols, 256), F32),
            buf((cols, 256), BF16),
            buf((cols, 256), BF16),
            buf((cols // 2, 256), BF16),
            buf((4, cols // 2, 256), BF16),
            buf((cols // 2, 256), BF16),
            buf((4, cols // 2, 256), BF16),
            buf((cols // 2, 256), BF16),
            buf((cols // 2, 256), BF16),
            buf((4, cols, own), BF16),
            buf((4, cols, own), BF16),
            buf((width, width), BF16),
            buf((own, width), F32),
            buf((own, width), BF16),
            buf((slots, own), BF16),
            buf((own, slots), BF16),
            buf((width, ff), BF16),
            buf((ff, width), BF16),
            buf((count, SLOT, width), BF16),
            buf((count, SLOT, width), BF16),
            buf((GROUP * SLOT, ff), BF16),
            buf((count, SLOT, width), BF16),
            buf((count, SLOT, width), BF16),
            dma((chunks,)),
            dma((4,)),
            dma((3,)),
            dma((3,)),
            dma((3,)),
            dma((3,)),
            dma((9,)),
            dma((9,)),
            dma((3,)),
            dma((4,)),
            dma((4,)),
            dma((4,)),
            dma((4,)),
            dma((2,)),
        ],
        compiler_params=pltpu.CompilerParams(
            collective_id=0, has_side_effects=True, vmem_limit_bytes=62 << 20
        ),
    )(
        tokens, w_query.T, w_key.T, w_value.T, freq, w_out, router, jnp.transpose(picks, (2, 1, 0)), w_in, w_down
    )


def solution(mesh):
    split = Mesh(mesh.devices.reshape(4, 4, 2, mesh.shape["head"]), AXES)
    seq = AXES[:3]
    in_specs = (
        P(seq, None),
        P(None, "head"),
        P(None, "head"),
        P(None, "head"),
        P(),
        P(),
        P(),
        P(AXES, None, None),
        P(AXES, None, None),
        P(None, AXES, None),
    )
    return jax.shard_map(
        per_device, mesh=split, in_specs=in_specs, out_specs=P(AXES, None), check_vma=False
    )
```

time: 110 us -> 89.3 us (0.81)
  Pallas kernels: 100 us -> 86.8 us
  local copies, waits for them, and re-layouts: 9.56 us -> 2.36 us
    pallas_call x2 -> x1, Pallas kernels: 100 us -> 86.8 us  [per_device(): pl.pallas_call(functools.partial(layer_kernel, cap), name='layer', out_sh...]
    unnamed x7 -> x1, local copies, waits for them, and re-layouts: 7.89 us -> 2.36 us
    reshape x2 -> x0, local copies, waits for them, and re-layouts: 1.67 us -> none  [the longest x1 0.98 us: experts(): padded.reshape(-1, 1)]
where the time goes in v1:
time: 89.3 us; the launch traced here: 89.1 us
  Pallas kernels  86.8 us (97%)
  local copies, waits for them, and re-layouts  2.36 us (3%)
    pallas_call x1, Pallas kernels, per_device(): pl.pallas_call(functools.partial(layer_kernel, cap), name='layer', out_sh...  86.8 us
    unnamed x1, local copies, waits for them, and re-layouts  2.36 us

profile of v1, /device:TPU:1, one launch (start us, length us, event | category | flops | bytes accessed | tf_op | source)
XLA Modules:
  0.0 89.1 jit_solution(13776838720612260137)
XLA Ops:
  0.0 86.8 %layer.1 = bf16[768,768]{1,0:T(8,128)(2,1)} custom-call(bf16[3072,768]{1,0:T(8,128)(2,1)} %tok.1, bf16[192,768]{1,0:T(8,128)(2,1)} %bitcast.4, bf16[192,768]{1,0:T(8,128)(2,1)} %bitcast.5, bf16[192,768]{1,0:T(8,128)(2,1)} %bitcast.6, f32[64,128]{1,0:T(8,128)} %freq.1, bf16[768,768]{1,0:T(8,128)(2,1)} %w_out.1, bf16[768,128]{1,0:T(8,128)(2,1)} %router.1, ...), custom_call_target="tpu_custom_call" | custom-call | tf_op jit(solution)/shard_map/layer/pallas_call | solution.py:375
  86.8 2.4 %copy.12 = bf16[768,768]{1,0:T(8,128)(2,1)} copy(bf16[768,768]{1,0:T(8,128)(2,1)} %layer.1) | data formatting | bytes 2359296

commit v2 on v1

--- a/solution.py
+++ b/solution.py
@@ -53,11 +53,14 @@
     return (SCALE - a * a).astype(BF16), (a * b).astype(BF16)
 
 
-def feature_heads(x, wx, wf01, wf2):
-    proj = nt(x, wx).astype(BF16)
+def phases(proj, wf01, wf2):
     pair, last = proj[:, :128], proj[:, 128:]
-    cos01, sin01 = waves(nn(jnp.concatenate([pair, pair], axis=1), wf01))
-    cos2, sin2 = waves(nn(last, wf2))
+    return nn(jnp.concatenate([pair, pair], axis=1), wf01), nn(last, wf2)
+
+
+def feature_heads(turns):
+    cos01, sin01 = waves(turns[0])
+    cos2, sin2 = waves(turns[1])
     return (
         jnp.concatenate([cos01[:, :128], sin01[:, :128]], axis=1),
         jnp.concatenate([cos01[:, 128:], sin01[:, 128:]], axis=1),
@@ -91,7 +94,7 @@
 
 def layer_kernel(
     cap, tok, wq, wk, wv, freq, w_out, router, picks, w_in, w_down, out,
-    xbuf, wqx, wkx, wf01, wf2, kf, qf, vt, before, intra, run, prefix,
+    xbuf, even, odd, wqx, wkx, wf01, wf2, kf, qf, vt, before, intra, run, prefix,
     cs, cr, ys, yr, zs, zr, fs, fr, att, slabs,
     wo, acc, hid, onehot, gates, first, second, outgoing, arrived, inner, result, returned,
     xsem, csem, ysend, yrecv, zsend, zrecv, hsend, hrecv, insem, osem, asem, rsem, bsem, lsem,
@@ -148,19 +151,42 @@
     wf2[64:128, :] = low
     run[...] = jnp.zeros_like(run)
 
-    @pl.loop(0, chunks // STEP)
+    last_chunk = chunks - 1
+
+    def project_key(i, ahead):
+        xs = xbuf[i]
+        ahead[...] = nt(xs, wkx[...]).astype(BF16)
+        vt[i] = nt(wv[...], xs).astype(BF16)
+
+    def store_key(i, turns):
+        for h, feats in enumerate(feature_heads(turns)):
+            kf[h, i] = feats
+
+    def absorb_key(i):
+        before[i] = run[...]
+        for h in range(heads):
+            band = slice(h * HD, (h + 1) * HD)
+            run[band, :] += nn(vt[i, band, :], kf[h, i])
+
+    fetch(0).wait()
+    project_key(0, even)
+
+    @pl.loop(0, chunks // 2)
     def _(p):
-        for i in [p * STEP + s for s in range(STEP)]:
-            fetch(i).wait()
-        for i in [p * STEP + s for s in range(STEP)]:
-            xs = xbuf[i]
-            vals = nt(wv[...], xs).astype(BF16)
-            vt[i] = vals
-            feats = feature_heads(xs, wkx[...], wf01[...], wf2[...])
-            before[i] = run[...]
-            for h in range(heads):
-                kf[h, i] = feats[h]
-                run[h * HD : (h + 1) * HD, :] += nn(vals[h * HD : (h + 1) * HD, :], feats[h])
+        fetch(2 * p + 1).wait()
+
+        @pl.when(2 * p + 2 <= last_chunk)
+        def _():
+            fetch(2 * p + 2).wait()
+
+        turns = phases(even[...], wf01[...], wf2[...])
+        project_key(2 * p + 1, odd)
+        store_key(2 * p, turns)
+        turns = phases(odd[...], wf01[...], wf2[...])
+        absorb_key(2 * p)
+        project_key(jnp.minimum(2 * p + 2, last_chunk), even)
+        store_key(2 * p + 1, turns)
+        absorb_key(2 * p + 1)
 
     def send(src, dst, ssem, rsem, to):
         return pltpu.make_async_remote_copy(
@@ -198,7 +224,22 @@
     columns = lax.broadcasted_iota(jnp.int32, (CHUNK, CHUNK), 1)
     causal = rows <= columns
 
-    @pl.loop(0, chunks // STEP)
+    def project_query(i, ahead):
+        ahead[...] = nt(xbuf[i], wqx[...]).astype(BF16)
+
+    def store_query(i, turns):
+        for h, feats in enumerate(feature_heads(turns)):
+            qf[h, i] = feats
+
+    def score(i):
+        for h in range(heads):
+            band = slice(h * HD, (h + 1) * HD)
+            scores = jnp.where(causal, nt(kf[h, i], qf[h, i]), 0.0).astype(BF16)
+            intra[i, band, :] = nn(vt[i, band, :], scores)
+
+    project_query(0, even)
+
+    @pl.loop(0, chunks // 2)
     def _(p):
         @pl.when(p == 1)
         def _():
@@ -219,14 +260,16 @@
             for copy in z_copies:
                 copy.start()
 
-        for i in [p * STEP + s for s in range(STEP)]:
-            feats = feature_heads(xbuf[i], wqx[...], wf01[...], wf2[...])
-            for h in range(heads):
-                qf[h, i] = feats[h]
-                scores = nt(kf[h, i], feats[h])
-                scores = jnp.where(causal, scores, 0.0).astype(BF16)
-                intra[i, h * HD : (h + 1) * HD, :] = nn(vt[i, h * HD : (h + 1) * HD, :], scores)
-
+        turns = phases(even[...], wf01[...], wf2[...])
+        score(jnp.maximum(2 * p - 1, 0))
+        project_query(2 * p + 1, odd)
+        store_query(2 * p, turns)
+        turns = phases(odd[...], wf01[...], wf2[...])
+        score(2 * p)
+        project_query(jnp.minimum(2 * p + 2, last_chunk), even)
+        store_query(2 * p + 1, turns)
+
+    score(last_chunk)
     for copy in z_copies:
         copy.wait()
     inside, _ = scan_pieces(zr, z)
@@ -356,7 +399,6 @@
     out[...] = (hid[...].astype(F32) + nn(gates[...], back)).astype(BF16)
 
 
-STEP = 2
 Y_DONE = 4
 
 
@@ -380,6 +422,8 @@
         out_specs=vmem,
         scratch_shapes=[
             buf((chunks, CHUNK, width), BF16),
+            buf((CHUNK, 256), BF16),
+            buf((CHUNK, 256), BF16),
             buf((256, width), BF16),
             buf((256, width), BF16),
             buf((256, 256), BF16),

time: 89.3 us -> 84.5 us (0.946)
  Pallas kernels: 86.8 us -> 82 us
    pallas_call x1, Pallas kernels: 86.8 us -> 82 us  [per_device(): pl.pallas_call(functools.partial(layer_kernel, cap), name='layer', out_sh...]
where the time goes in v2:
time: 84.5 us; the launch traced here: 84.4 us
  Pallas kernels  82 us (97%)
  local copies, waits for them, and re-layouts  2.36 us (3%)
    pallas_call x1, Pallas kernels, per_device(): pl.pallas_call(functools.partial(layer_kernel, cap), name='layer', out_sh...  82 us
    unnamed x1, local copies, waits for them, and re-layouts  2.36 us

profile of v2, /device:TPU:1, one launch (start us, length us, event | category | flops | bytes accessed | tf_op | source)
XLA Modules:
  0.0 84.4 jit_solution(10792132635399305838)
XLA Ops:
  0.0 82.0 %layer.1 = bf16[768,768]{1,0:T(8,128)(2,1)} custom-call(bf16[3072,768]{1,0:T(8,128)(2,1)} %tok.1, bf16[192,768]{1,0:T(8,128)(2,1)} %bitcast.4, bf16[192,768]{1,0:T(8,128)(2,1)} %bitcast.5, bf16[192,768]{1,0:T(8,128)(2,1)} %bitcast.6, f32[64,128]{1,0:T(8,128)} %freq.1, bf16[768,768]{1,0:T(8,128)(2,1)} %w_out.1, bf16[768,128]{1,0:T(8,128)(2,1)} %router.1, ...), custom_call_target="tpu_custom_call" | custom-call | tf_op jit(solution)/shard_map/layer/pallas_call | solution.py:417
  82.0 2.4 %copy.12 = bf16[768,768]{1,0:T(8,128)(2,1)} copy(bf16[768,768]{1,0:T(8,128)(2,1)} %layer.1) | data formatting | bytes 2359296

commit v3 on v2

--- a/solution.py
+++ b/solution.py
@@ -86,6 +86,7 @@
 
 
 ORDER = message_order()
+CODES = [((f[0] * 4 + f[1]) * 2 + f[2]) * 4 + f[3] for f in ORDER]
 
 
 def flat(p):
@@ -93,7 +94,7 @@
 
 
 def layer_kernel(
-    cap, tok, wq, wk, wv, freq, w_out, router, picks, w_in, w_down, out,
+    cap, tok, wq, wk, wv, freq, w_out, router, picks, codes, w_in, w_down, out,
     xbuf, even, odd, wqx, wkx, wf01, wf2, kf, qf, vt, before, intra, run, prefix,
     cs, cr, ys, yr, zs, zr, fs, fr, att, slabs,
     wo, acc, hid, onehot, gates, first, second, outgoing, arrived, inner, result, returned,
@@ -306,8 +307,11 @@
         finish(x * per + j, j, slabs.at[x])
 
     numbers = jnp.concatenate([picks[...].reshape(cap, count), jnp.full((SLOT - cap, count), -16, jnp.int32)], axis=0)
-    big = (numbers >> 4).astype(F32).astype(BF16)
-    small = (numbers & 15).astype(F32).astype(BF16)
+    me = flat((z, y, c, x))
+    ordered = lax.broadcasted_iota(jnp.int32, (count, count), 0) == (codes[...] ^ me)
+    ordered = ordered.astype(F32).astype(BF16)
+    big = nn((numbers >> 4).astype(F32).astype(BF16), ordered).astype(BF16)
+    small = nn((numbers & 15).astype(F32).astype(BF16), ordered).astype(BF16)
     tall = lax.broadcasted_iota(jnp.int32, (slots, count), 0) >> 3
     tall = (tall == lax.broadcasted_iota(jnp.int32, (slots, count), 1)).astype(F32).astype(BF16)
     places = nt(tall, big) * 16.0 + nt(tall, small)
@@ -340,8 +344,6 @@
         h_copies[2, j].wait()
     hid[...] = (acc[...] + project(2)).astype(BF16)
 
-    me = flat((z, y, c, x))
-
     def drain(src, dst, ssem, rsem, g, sent):
         n = GROUP - 1 if g == 3 else GROUP
         copy = send(
@@ -356,22 +358,21 @@
         else:
             copy.wait_recv()
 
-    own_out = pltpu.make_async_copy(outgoing.at[me], arrived.at[count - 1], lsem.at[0])
-    own_back = pltpu.make_async_copy(result.at[count - 1], returned.at[me], lsem.at[1])
+    own_out = pltpu.make_async_copy(outgoing.at[count - 1], arrived.at[count - 1], lsem.at[0])
+    own_back = pltpu.make_async_copy(result.at[count - 1], returned.at[count - 1], lsem.at[1])
 
     for b in range(slots // span):
         rows = nn(onehot[b * span : (b + 1) * span, :], hid[...])
         outgoing[b * GROUP : (b + 1) * GROUP] = rows.reshape(GROUP, SLOT, width).astype(BF16)
-    for i in range(count - 1):
-        p = peer(ORDER[i])
-        g = i // GROUP
-        send(
-            outgoing.at[flat(p), pl.ds(0, cap)], arrived.at[i, pl.ds(0, cap)], osem.at[g], asem.at[g], p
-        ).start()
+        for i in range(b * GROUP, min((b + 1) * GROUP, count - 1)):
+            send(
+                outgoing.at[i, pl.ds(0, cap)], arrived.at[i, pl.ds(0, cap)], osem.at[b], asem.at[b], peer(ORDER[i])
+            ).start()
     own_out.start()
 
     gate = jax.nn.sigmoid(nn(hid[...], router[...])).astype(BF16)
     matched = lax.broadcasted_iota(jnp.int32, (tokens, slots), 0) == pick_row
+    gate = nn(gate, ordered).astype(BF16)
     gates[...] = jnp.where(matched, nn(gate, wide), 0.0).astype(BF16)
 
     first_copy.wait()
@@ -387,16 +388,22 @@
         result[group] = nn(inner[...], second[...]).reshape(GROUP, SLOT, width).astype(BF16)
         for i in range(g * GROUP, min((g + 1) * GROUP, count - 1)):
             send(
-                result.at[i, pl.ds(0, cap)], returned.at[me, pl.ds(0, cap)], bsem.at[g], rsem.at[g], peer(ORDER[i])
+                result.at[i, pl.ds(0, cap)], returned.at[i, pl.ds(0, cap)], bsem.at[g], rsem.at[g], peer(ORDER[i])
             ).start()
     own_back.start()
     own_back.wait()
-    for g in range(4):
-        drain(outgoing, arrived, osem, asem, g, True)
-        drain(result, returned, bsem, rsem, g, True)
-        drain(result, returned, bsem, rsem, g, False)
-    back = returned[...].astype(F32).reshape(slots, width).astype(BF16)
-    out[...] = (hid[...].astype(F32) + nn(gates[...], back)).astype(BF16)
+
+    def combine(groups):
+        for g in groups:
+            drain(outgoing, arrived, osem, asem, g, True)
+            drain(result, returned, bsem, rsem, g, True)
+            drain(result, returned, bsem, rsem, g, False)
+        first_row, end = groups[0] * GROUP, (groups[-1] + 1) * GROUP
+        back = returned[first_row:end].astype(F32).reshape((end - first_row) * SLOT, width).astype(BF16)
+        return nn(gates[:, first_row * SLOT : end * SLOT], back)
+
+    acc[...] = hid[...].astype(F32) + combine((0, 1, 2))
+    out[...] = (acc[...] + combine((3,))).astype(BF16)
 
 
 Y_DONE = 4
@@ -418,7 +425,7 @@
         functools.partial(layer_kernel, cap),
         name="layer",
         out_shape=jax.ShapeDtypeStruct((own, width), BF16),
-        in_specs=[hbm] + [vmem] * 4 + [hbm] + [vmem] * 2 + [hbm] * 2,
+        in_specs=[hbm] + [vmem] * 4 + [hbm] + [vmem] * 3 + [hbm] * 2,
         out_specs=vmem,
         scratch_shapes=[
             buf((chunks, CHUNK, width), BF16),
@@ -476,7 +483,17 @@
             collective_id=0, has_side_effects=True, vmem_limit_bytes=62 << 20
         ),
     )(
-        tokens, w_query.T, w_key.T, w_value.T, freq, w_out, router, jnp.transpose(picks, (2, 1, 0)), w_in, w_down
+        tokens,
+        w_query.T,
+        w_key.T,
+        w_value.T,
+        freq,
+        w_out,
+        router,
+        jnp.transpose(picks, (2, 1, 0)),
+        jnp.asarray(CODES, jnp.int32).reshape(1, count),
+        w_in,
+        w_down,
     )
 
 

time: 84.5 us -> 84.7 us (level)
  no operation moved by 1% of the time
where the time goes in v3:
time: 84.7 us; the launch traced here: 84.5 us
  Pallas kernels  82.2 us (97%)
  local copies, waits for them, and re-layouts  2.36 us (3%)
    pallas_call x1, Pallas kernels, per_device(): pl.pallas_call(functools.partial(layer_kernel, cap), name='layer', out_sh...  82.2 us
    unnamed x1, local copies, waits for them, and re-layouts  2.36 us

profile of v3, /device:TPU:1, one launch (start us, length us, event | category | flops | bytes accessed | tf_op | source)
XLA Modules:
  0.0 84.5 jit_solution(8005773485544835640)
XLA Ops:
  0.0 82.2 %layer.1 = bf16[768,768]{1,0:T(8,128)(2,1)} custom-call(bf16[3072,768]{1,0:T(8,128)(2,1)} %tok.1, bf16[192,768]{1,0:T(8,128)(2,1)} %bitcast.4, bf16[192,768]{1,0:T(8,128)(2,1)} %bitcast.5, bf16[192,768]{1,0:T(8,128)(2,1)} %bitcast.6, f32[64,128]{1,0:T(8,128)} %freq.1, bf16[768,768]{1,0:T(8,128)(2,1)} %w_out.1, bf16[768,128]{1,0:T(8,128)(2,1)} %router.1, ...), custom_call_target="tpu_custom_call" | custom-call | tf_op jit(solution)/shard_map/layer/pallas_call | solution.py:424
  82.2 2.4 %copy.13 = bf16[768,768]{1,0:T(8,128)(2,1)} copy(bf16[768,768]{1,0:T(8,128)(2,1)} %layer.1) | data formatting | bytes 2359296

commit v4 on v3

--- a/solution.py
+++ b/solution.py
@@ -128,14 +128,8 @@
     returned[...] = jnp.zeros_like(returned)
     barrier = pltpu.get_barrier_semaphore()
 
-    @pl.loop(1, 128)
-    def _(k):
-        pl.semaphore_signal(
-            barrier,
-            inc=1,
-            device_id=(z ^ (k & 3), y ^ ((k >> 2) & 3), c ^ (k >> 6), x ^ ((k >> 4) & 3)),
-            device_id_type=MESH,
-        )
+    for offset in ORDER[:-1]:
+        pl.semaphore_signal(barrier, inc=1, device_id=peer(offset), device_id_type=MESH)
 
     for src, dst in ((wq, wqx), (wk, wkx)):
         dst[:192, :] = src[...]
@@ -407,6 +401,20 @@
 
 
 Y_DONE = 4
+PIECES = 4
+
+
+def hand_over_kernel(src, dst, buf, isem, osem):
+    rows = buf.shape[1]
+    arrive = [pltpu.make_async_copy(src.at[i * rows : (i + 1) * rows], buf.at[i], isem.at[i]) for i in range(PIECES)]
+    leave = [pltpu.make_async_copy(buf.at[i], dst.at[i * rows : (i + 1) * rows], osem.at[i]) for i in range(PIECES)]
+    for copy in arrive:
+        copy.start()
+    for i in range(PIECES):
+        arrive[i].wait()
+        leave[i].start()
+    for copy in leave:
+        copy.wait()
 
 
 def per_device(tokens, w_query, w_key, w_value, freq, w_out, router, w_in, w_down, picks):
@@ -421,7 +429,7 @@
     hbm = pl.BlockSpec(memory_space=pl.ANY)
     dma = pltpu.SemaphoreType.DMA
     buf = pltpu.VMEM
-    return pl.pallas_call(
+    result = pl.pallas_call(
         functools.partial(layer_kernel, cap),
         name="layer",
         out_shape=jax.ShapeDtypeStruct((own, width), BF16),
@@ -495,6 +503,14 @@
         w_in,
         w_down,
     )
+    return pl.pallas_call(
+        hand_over_kernel,
+        name="hand_over",
+        out_shape=jax.ShapeDtypeStruct(result.shape, result.dtype),
+        in_specs=[hbm],
+        out_specs=hbm,
+        scratch_shapes=[buf((PIECES, own // PIECES, width), BF16), dma((PIECES,)), dma((PIECES,))],
+    )(result)
 
 
 def solution(mesh):

time: 84.7 us -> 83.4 us (0.985)
  local copies, waits for them, and re-layouts: 2.36 us -> 0 us
  Pallas kernels: 82.2 us -> 83.1 us
    unnamed x1 -> x0, local copies, waits for them, and re-layouts: 2.36 us -> none
    pallas_call x0 -> x1, Pallas kernels: none -> 2.04 us  [per_device(): pl.pallas_call(hand_over_kernel, name='hand_over', out_shape=jax.ShapeDty...]
    pallas_call x1, Pallas kernels: 82.2 us -> 81 us  [per_device(): pl.pallas_call(functools.partial(layer_kernel, cap), name='layer', out_sh...]
where the time goes in v4:
time: 83.4 us; the launch traced here: 83.2 us
  Pallas kernels  83.1 us (100%)
    pallas_call x1, Pallas kernels, per_device(): pl.pallas_call(functools.partial(layer_kernel, cap), name='layer', out_sh...  81 us
    pallas_call x1, Pallas kernels, per_device(): pl.pallas_call(hand_over_kernel, name='hand_over', out_shape=jax.ShapeDty...  2.04 us

profile of v4, /device:TPU:1, one launch (start us, length us, event | category | flops | bytes accessed | tf_op | source)
XLA Modules:
  0.0 83.2 jit_solution(17688373628199621698)
XLA Ops:
  0.0 81.0 %layer.1.src = bf16[768,768]{1,0:T(8,128)(2,1)} custom-call(bf16[3072,768]{1,0:T(8,128)(2,1)} %tok.1, bf16[192,768]{1,0:T(8,128)(2,1)} %bitcast.4, bf16[192,768]{1,0:T(8,128)(2,1)} %bitcast.5, bf16[192,768]{1,0:T(8,128)(2,1)} %bitcast.6, f32[64,128]{1,0:T(8,128)} %freq.1, bf16[768,768]{1,0:T(8,128)(2,1)} %w_out.1, bf16[768,128]{1,0:T(8,128)(2,1)} %router.1, ...), custom_call_target="tpu_custom_call" | custom-call | tf_op jit(solution)/shard_map/layer/pallas_call | solution.py:432
  81.0 2.0 %hand_over.1 = bf16[768,768]{1,0:T(8,128)(2,1)} custom-call(bf16[768,768]{1,0:T(8,128)(2,1)} %layer.1.src), custom_call_target="tpu_custom_call" | custom-call | tf_op jit(solution)/shard_map/hand_over/pallas_call | solution.py:506

commit v5 on v4

--- a/solution.py
+++ b/solution.py
@@ -71,6 +71,8 @@
 SLOT = 8
 GROUP = 32
 HOPS = (0, 1, 2, 1)
+PARTS = ((0, 48), (48, 96), (96, 128))
+PART_OF = [g for g, (low, high) in enumerate(PARTS) for _ in range(low, high)]
 
 
 def message_order():
@@ -339,7 +341,7 @@
     hid[...] = (acc[...] + project(2)).astype(BF16)
 
     def drain(src, dst, ssem, rsem, g, sent):
-        n = GROUP - 1 if g == 3 else GROUP
+        n = min(PARTS[g][1], count - 1) - PARTS[g][0]
         copy = send(
             src.at[pl.ds(0, n), pl.ds(0, cap)],
             dst.at[pl.ds(0, n), pl.ds(0, cap)],
@@ -360,7 +362,8 @@
         outgoing[b * GROUP : (b + 1) * GROUP] = rows.reshape(GROUP, SLOT, width).astype(BF16)
         for i in range(b * GROUP, min((b + 1) * GROUP, count - 1)):
             send(
-                outgoing.at[i, pl.ds(0, cap)], arrived.at[i, pl.ds(0, cap)], osem.at[b], asem.at[b], peer(ORDER[i])
+                outgoing.at[i, pl.ds(0, cap)], arrived.at[i, pl.ds(0, cap)], osem.at[PART_OF[i]],
+                asem.at[PART_OF[i]], peer(ORDER[i])
             ).start()
     own_out.start()
 
@@ -372,15 +375,15 @@
     first_copy.wait()
     second_copy.wait()
     own_out.wait()
-    for g in range(4):
+    for g, (low, high) in enumerate(PARTS):
         drain(outgoing, arrived, osem, asem, g, False)
-        group = slice(g * GROUP, (g + 1) * GROUP)
-        rows = arrived[group].astype(F32).reshape(span, width).astype(BF16)
+        part_rows = (high - low) * SLOT
+        rows = arrived[low:high].astype(F32).reshape(part_rows, width).astype(BF16)
         for part in range(6):
             band = slice(part * 512, (part + 1) * 512)
-            inner[:, band] = jax.nn.gelu(nn(rows, first[:, band]), approximate=True).astype(BF16)
-        result[group] = nn(inner[...], second[...]).reshape(GROUP, SLOT, width).astype(BF16)
-        for i in range(g * GROUP, min((g + 1) * GROUP, count - 1)):
+            inner[:part_rows, band] = jax.nn.gelu(nn(rows, first[:, band]), approximate=True).astype(BF16)
+        result[low:high] = nn(inner[:part_rows, :], second[...]).reshape(high - low, SLOT, width).astype(BF16)
+        for i in range(low, min(high, count - 1)):
             send(
                 result.at[i, pl.ds(0, cap)], returned.at[i, pl.ds(0, cap)], bsem.at[g], rsem.at[g], peer(ORDER[i])
             ).start()
@@ -392,12 +395,12 @@
             drain(outgoing, arrived, osem, asem, g, True)
             drain(result, returned, bsem, rsem, g, True)
             drain(result, returned, bsem, rsem, g, False)
-        first_row, end = groups[0] * GROUP, (groups[-1] + 1) * GROUP
+        first_row, end = PARTS[groups[0]][0], PARTS[groups[-1]][1]
         back = returned[first_row:end].astype(F32).reshape((end - first_row) * SLOT, width).astype(BF16)
         return nn(gates[:, first_row * SLOT : end * SLOT], back)
 
-    acc[...] = hid[...].astype(F32) + combine((0, 1, 2))
-    out[...] = (acc[...] + combine((3,))).astype(BF16)
+    acc[...] = hid[...].astype(F32) + combine((0, 1))
+    out[...] = (acc[...] + combine((2,))).astype(BF16)
 
 
 Y_DONE = 4
@@ -469,7 +472,7 @@
             buf((ff, width), BF16),
             buf((count, SLOT, width), BF16),
             buf((count, SLOT, width), BF16),
-            buf((GROUP * SLOT, ff), BF16),
+            buf((48 * SLOT, ff), BF16),
             buf((count, SLOT, width), BF16),
             buf((count, SLOT, width), BF16),
             dma((chunks,)),

time: 83.4 us -> 84.1 us (level)
  no operation moved by 1% of the time
where the time goes in v5:
time: 84.1 us; the launch traced here: 84 us
  Pallas kernels  83.8 us (100%)
    pallas_call x1, Pallas kernels, per_device(): pl.pallas_call(functools.partial(layer_kernel, cap), name='layer', out_sh...  81.8 us
    pallas_call x1, Pallas kernels, per_device(): pl.pallas_call(hand_over_kernel, name='hand_over', out_shape=jax.ShapeDty...  2.04 us

profile of v5, /device:TPU:1, one launch (start us, length us, event | category | flops | bytes accessed | tf_op | source)
XLA Modules:
  0.0 84.0 jit_solution(13895326442593218601)
XLA Ops:
  0.0 81.8 %layer.1.src = bf16[768,768]{1,0:T(8,128)(2,1)} custom-call(bf16[3072,768]{1,0:T(8,128)(2,1)} %tok.1, bf16[192,768]{1,0:T(8,128)(2,1)} %bitcast.4, bf16[192,768]{1,0:T(8,128)(2,1)} %bitcast.5, bf16[192,768]{1,0:T(8,128)(2,1)} %bitcast.6, f32[64,128]{1,0:T(8,128)} %freq.1, bf16[768,768]{1,0:T(8,128)(2,1)} %w_out.1, bf16[768,128]{1,0:T(8,128)(2,1)} %router.1, ...), custom_call_target="tpu_custom_call" | custom-call | tf_op jit(solution)/shard_map/layer/pallas_call | solution.py:435
  81.8 2.0 %hand_over.1 = bf16[768,768]{1,0:T(8,128)(2,1)} custom-call(bf16[768,768]{1,0:T(8,128)(2,1)} %layer.1.src), custom_call_target="tpu_custom_call" | custom-call | tf_op jit(solution)/shard_map/hand_over/pallas_call | solution.py:509
